TPU v7x, 256 devices: a whole 4x4x8 slice. The times are simulated.
256 devices in a mesh: store: 32 (over y, z), tp: 8 (over x, core).
Axes of the slice: x: 4, y: 4, z: 8, core: 2. Of those that a mesh axis runs over, the one named last changes fastest.
Arguments:
- queries: bfloat16 [32768, 8192], P('store', 'tp')
- fresh_kv: bfloat16 [2, 32768, 1024], P(None, ('store', 'tp'))
- page_pool: bfloat16 [2048, 2, 128, 1024], P('store', None, None, 'tp')
- page_host: int32 [128, 8], P('store'), may hold values from 0 to 31, as said below
- page_slot: int32 [128, 8], P('store'), may hold values from 0 to 63, as said below
- prefix_len: int32 [128], P('store'), may hold values from 513 to 1024
- fresh_len: int32 [32, 4], P('store'), may hold values from 1 to 384, 1024 in all within a row
Outputs:
- attention: bfloat16 [32768, 8192], P('store', 'tp')
Inputs may be any that keep to these rules, and one draw needn't show every extreme that they name: `page_host`: page p of request r is read only if p < ceil(prefix_len[r] / 128). Among the pages read by the 4 requests of one host, at most 2 lie on any one host; in every draw some host holds exactly 2 of the pages read by each host. `page_slot`: several entries may name the same stored page. `fresh_len`: the requests of a host own consecutive rows of its block, in order.
All inputs are finite; a program needn't handle non-finite values.
Results may differ from a plain program's by a relative error of at most 0.0041.
Values may be sent and summed in bfloat16 or wider, within the bound.
A program may use at most 128 MiB of HBM per device.

v0:
```python
import math
import jax
import jax.numpy as jnp
from jax import lax
from jax.sharding import PartitionSpec as P

HD = 128
REQ_HOST = 4
PAGE = 128
PAGES_MAX = 8
MOST_NEW = 384


def plan_requests(owners, slot_ids, prefix, stores, capacity):
    entry_count = owners.shape[0] * owners.shape[1]
    page_count = (prefix + PAGE - 1) // PAGE
    in_use = (jnp.arange(owners.shape[1], dtype=jnp.int32)[None, :] < page_count[:, None]).reshape(
        entry_count
    )
    flat_owners = owners.reshape(entry_count)
    flat_slots = slot_ids.reshape(entry_count)
    entries = jnp.arange(entry_count, dtype=jnp.int32)
    same_owner = (
        (flat_owners[:, None] == flat_owners[None, :])
        & in_use[None, :]
        & (entries[None, :] < entries[:, None])
    )
    owner_rank = jnp.sum(same_owner.astype(jnp.int32), axis=1)
    position = jnp.where(in_use, flat_owners * capacity + owner_rank, 0)
    target = jnp.arange(stores * capacity, dtype=jnp.int32)
    matches = (position[:, None] == target[None, :]) & in_use[:, None]
    buffer = jnp.sum(jnp.where(matches, flat_slots[:, None], 0), axis=0)
    return (buffer.reshape(stores, capacity), position)


def attend(q_rows, key_rows, value_rows, key_valid):
    scores = jnp.einsum("mkgd,nkd->kgmn", q_rows, key_rows, preferred_element_type=jnp.float32) * (
        1.0 / math.sqrt(HD)
    )
    row_top = jnp.max(jnp.where(key_valid, scores, -1e30), axis=-1, keepdims=True)
    weights = jnp.where(key_valid, jnp.exp(scores - row_top), 0.0)
    row_total = jnp.sum(weights, axis=-1)
    rounded = weights.astype(jnp.bfloat16)
    mixed_rows = jnp.einsum(
        "kgmn,nkd->mkgd", rounded, value_rows, preferred_element_type=jnp.float32
    )
    return (mixed_rows / jnp.transpose(row_total, (2, 0, 1))[..., None]).astype(jnp.bfloat16)


def local(queries, fresh_kv, page_pool, page_host, page_slot, prefix_len, fresh_len):
    stores = lax.axis_size("store")
    block_rows = queries.shape[0]
    head_width = page_pool.shape[3]
    kv_local = head_width // HD
    group_size = queries.shape[1] // head_width
    capacity = max(2, (REQ_HOST * PAGES_MAX + stores - 1) // stores)
    gathered = lax.all_gather(fresh_kv, "tp", axis=1, tiled=True)
    new_kv = lax.dynamic_slice_in_dim(gathered, lax.axis_index("tp") * head_width, head_width, 2)
    buffer, position = plan_requests(page_host, page_slot, prefix_len, stores, capacity)
    arrived = lax.all_to_all(
        jnp.take(
            page_pool,
            lax.all_to_all(buffer, "store", split_axis=0, concat_axis=0, tiled=True),
            axis=0,
        ),
        "store",
        split_axis=0,
        concat_axis=0,
        tiled=True,
    )
    flat_pages = arrived.reshape(stores * capacity, 2, PAGE, head_width)
    fetched = jnp.take(flat_pages, position, axis=0).reshape(
        REQ_HOST, PAGES_MAX, 2, PAGE, head_width
    )
    lengths = fresh_len[0]
    offsets = jnp.cumsum(lengths) - lengths
    positions = jnp.arange(MOST_NEW, dtype=jnp.int32)
    cache_index = jnp.arange(PAGES_MAX * PAGE, dtype=jnp.int32)
    output = jnp.zeros_like(queries)
    for request in range(REQ_HOST):
        offset = offsets[request]
        length = lengths[request]
        window_start = jnp.minimum(offset, block_rows - MOST_NEW)
        q_rows = lax.dynamic_slice_in_dim(queries, window_start, MOST_NEW, 0).reshape(
            MOST_NEW, kv_local, group_size, HD
        )
        new_rows = lax.dynamic_slice_in_dim(new_kv, window_start, MOST_NEW, 1).reshape(
            2, MOST_NEW, kv_local, HD
        )
        cached_keys = fetched[request, :, 0].reshape(PAGES_MAX * PAGE, kv_local, HD)
        cached_values = fetched[request, :, 1].reshape(PAGES_MAX * PAGE, kv_local, HD)
        key_rows = jnp.concatenate([cached_keys, new_rows[0]], axis=0)
        value_rows = jnp.concatenate([cached_values, new_rows[1]], axis=0)
        query_pos = window_start + positions
        cache_ok = jnp.broadcast_to(
            cache_index[None, :] < prefix_len[request], (MOST_NEW, PAGES_MAX * PAGE)
        )
        fresh_ok = (query_pos[None, :] >= offset) & (query_pos[None, :] <= query_pos[:, None])
        key_valid = jnp.concatenate([cache_ok, fresh_ok], axis=1)
        mixed_rows = attend(q_rows, key_rows, value_rows, key_valid).reshape(
            MOST_NEW, queries.shape[1]
        )
        row_ok = (query_pos >= offset) & (query_pos < offset + length)
        old_rows = lax.dynamic_slice_in_dim(output, window_start, MOST_NEW, 0)
        output = lax.dynamic_update_slice_in_dim(
            output, jnp.where(row_ok[:, None], mixed_rows, old_rows), window_start, 0
        )
    return output


def solution(mesh):
    placed = (
        P("store", "tp"),
        P(None, ("store", "tp"), None),
        P("store", None, None, "tp"),
        P("store", None),
        P("store", None),
        P("store"),
        P("store", None),
    )
    return jax.shard_map(
        local, mesh=mesh, in_specs=placed, out_specs=P("store", "tp"), check_vma=False
    )
```

profile of v0, /device:TPU:2, one launch (start us, length us, event | category | flops | bytes accessed | tf_op | source)
XLA Modules:
  0.0 311.5 jit_solution(1080985737066531450)
XLA Ops:
  9.4 21.1 %all_to_all.20 = s32[32,1,2]{2,1,0:T(1,128)S(1)} all-to-all(s32[32,1,2]{2,1,0:T(1,128)S(1)} %bitcast.273), channel_id=1, replica_groups=mesh['store'=32,'tp'=8] {'store'}, dimensions={0} | all-to-all | bytes 512 | tf_op jit(solution)/shard_map/all_to_all | solution.py:63
  30.9 5.3 %gather_fusion = bf16[64,2,128,128]{3,2,1,0:T(8,128)(2,1)} fusion(bf16[64,2,128,128]{3,2,1,0:T(8,128)(2,1)} %param.9, s32[1024]{0:T(1024)S(1)} %pad_clamp_fusion.1), kind=kCustom, calls=%fused_computation | custom fusion | bytes 8388864 | tf_op jit(solution)/shard_map/jit(_take)/gather | solution.py:61
  36.2 4.5 %broadcast_select_fusion = bf16[32,2,2,128,128]{4,3,2,1,0:T(8,128)(2,1)} fusion(bf16[32,2,2,128,128]{4,3,2,1,0:T(8,128)(2,1)} %bitcast.255, pred[32,2]{1,0:T(8,128)(4,1)S(1)} %copy.87), kind=kLoop, calls=%fused_computation.42 | loop fusion | flops 2097152 | bytes 8388672 | tf_op jit(solution)/shard_map/jit(_take)/select_n | solution.py:61
  40.7 4.9 %all-to-all-start.1 = ((bf16[32,2,2,128,128]{4,3,2,1,0:T(8,128)(2,1)}), bf16[32,2,2,128,128]{4,3,2,1,0:T(8,128)(2,1)}, u32[]{:S(2)}, u32[]{:S(2)}) async-start(bf16[32,2,2,128,128]{4,3,2,1,0:T(8,128)(2,1)} %broadcast_select_fusion), calls=%async_computation.1 | async-start | bytes 8388608 | tf_op jit(solution)/shard_map/all_to_all | solution.py:60
  49.8 2.1 constant_dynamic-slice_fusion
  51.9 2.3 copy.129
  56.3 2.4 copy.128
  72.7 10.4 %all-gather.2.cloned.1.call-done = bf16[2,1024,1024]{2,1,0:T(8,128)(2,1)} async-done(((bf16[2,128,1024]{2,1,0:T(8,128)(2,1)}), bf16[2,1024,1024]{2,1,0:T(8,128)(2,1)}) %all-gather.2.cloned.1.call-update) | async-done | bytes 4194320 | tf_op jit(solution)/shard_map/all_gather | solution.py:57
  83.1 2.8 dynamic-slice_bitcast_fusion.1
  88.9 52.7 %all-to-all-done.1 = bf16[32,2,2,128,128]{4,3,2,1,0:T(8,128)(2,1)} async-done(((bf16[32,2,2,128,128]{4,3,2,1,0:T(8,128)(2,1)}), bf16[32,2,2,128,128]{4,3,2,1,0:T(8,128)(2,1)}, u32[]{:S(2)}, u32[]{:S(2)}) %all-to-all-start.1) | async-done | bytes 4194336 | tf_op jit(solution)/shard_map/all_to_all | solution.py:60
  141.6 4.3 %gather_fusion.1 = bf16[32,2,128,128]{3,2,1,0:T(8,128)(2,1)} fusion(bf16[64,2,128,128]{3,2,1,0:T(8,128)(2,1)} %bitcast.9, s32[1024]{0:T(1024)S(1)} %pad_clamp_fusion), kind=kCustom, calls=%fused_computation.1 | custom fusion | bytes 4194432 | tf_op jit(solution)/shard_map/jit(_take)/gather | solution.py:72
  145.9 1.8 broadcast_select_fusion.1
  150.7 9.9 %fusion = (f32[8,384]{1,0:T(8,128)S(1)}, f32[1408,384,8]{1,0,2:T(8,128)}) fusion(pred[384,1408]{0,1:T(8,128)(4,1)S(1)} %pad_add_fusion.3, bf16[384,8,128]{0,2,1:T(8,128)(2,1)} %bitcast.260, bf16[384,1,128]{2,0,1:T(8,128)(2,1)} %get-tuple-element.9, bf16[1024,1,128]{2,0,1:T(8,128)(2,1)} %bitcast.264), kind=kOutput, calls=%fused_computation.4 | convolution fusion | flops 1120990208 | bytes 19001344 | tf_op jit(solution)/shard_map/mkgd,nkd->kgmn/dot_general | solution.py:37
  160.6 9.8 %fusion.18 = f32[8,384]{1,0:T(8,128)S(1)} fusion(f32[1408,384,8]{1,0,2:T(8,128)} %get-tuple-element.44, f32[8,384]{1,0:T(8,128)S(1)} %get-tuple-element.43, pred[384,1408]{0,1:T(8,128)(4,1)S(1)} %pad_add_fusion.3), kind=kLoop, calls=%fused_computation.28 | loop fusion | flops 17298432 | bytes 17866752 | tf_op jit(solution)/shard_map/reduce_sum | solution.py:42
  170.5 10.7 %fusion.36 = bf16[384,1,8,128]{0,3,2,1:T(8,128)(2,1)} fusion(f32[1408,384,8]{1,0,2:T(8,128)} %get-tuple-element.44, f32[8,384]{1,0:T(8,128)S(1)} %get-tuple-element.43, pred[384,1408]{0,1:T(8,128)(4,1)S(1)} %pad_add_fusion.3, f32[384,8]{0,1:T(8,128)S(1)} %bitcast.274, bf16[384,1,128]{0,2,1:T(8,128)(2,1)} %copy.109, bf16[1024,1,128]{0,2,1:T(8,128)(2,1)} %copy.125), kind=kOutput, calls=%fused_computation.49 | convolution fusion | flops 1126105088 | bytes 19013632 | tf_op jit(solution)/shard_map/kgmn,nkd->mkgd/dot_general | solution.py:44
  181.1 2.3 copy.113
  185.2 9.9 %fusion.3 = (f32[8,384]{1,0:T(8,128)S(1)}, f32[1408,384,8]{1,0,2:T(8,128)}) fusion(pred[384,1408]{0,1:T(8,128)(4,1)S(1)} %pad_add_fusion.2, bf16[384,8,128]{0,2,1:T(8,128)(2,1)} %bitcast.259, bf16[384,1,128]{2,0,1:T(8,128)(2,1)} %get-tuple-element.10, bf16[1024,1,128]{2,0,1:T(8,128)(2,1)} %bitcast.263), kind=kOutput, calls=%fused_computation.9 | convolution fusion | flops 1120990208 | bytes 19001344 | tf_op jit(solution)/shard_map/mkgd,nkd->kgmn/dot_general | solution.py:37
  195.2 9.4 %fusion.16 = f32[8,384]{1,0:T(8,128)S(1)} fusion(f32[1408,384,8]{1,0,2:T(8,128)} %get-tuple-element.42, f32[8,384]{1,0:T(8,128)S(1)} %get-tuple-element.41, pred[384,1408]{0,1:T(8,128)(4,1)S(1)} %pad_add_fusion.2), kind=kLoop, calls=%fused_computation.26 | loop fusion | flops 17298432 | bytes 17866752 | tf_op jit(solution)/shard_map/reduce_sum | solution.py:42
  204.6 10.8 %fusion.37 = bf16[384,1,8,128]{0,3,2,1:T(8,128)(2,1)} fusion(f32[1408,384,8]{1,0,2:T(8,128)} %get-tuple-element.42, f32[8,384]{1,0:T(8,128)S(1)} %get-tuple-element.41, pred[384,1408]{0,1:T(8,128)(4,1)S(1)} %pad_add_fusion.2, f32[384,8]{0,1:T(8,128)S(1)} %bitcast.275, bf16[384,1,128]{0,2,1:T(8,128)(2,1)S(1)} %copy-done.9, bf16[1024,1,128]{0,2,1:T(8,128)(2,1)} %copy.124), kind=kOutput, calls=%fused_computation.51 | convolution fusion | flops 1126105088 | bytes 19013632 | tf_op jit(solution)/shard_map/kgmn,nkd->mkgd/dot_general | solution.py:44
  215.4 2.3 copy.107
  218.6 8.9 %fusion.6 = (f32[8,384]{1,0:T(8,128)S(1)}, f32[1408,384,8]{1,0,2:T(8,128)}) fusion(pred[384,1408]{0,1:T(8,128)(4,1)S(1)} %pad_add_fusion.1, bf16[384,8,128]{0,2,1:T(8,128)(2,1)} %bitcast.258, bf16[384,1,128]{2,0,1:T(8,128)(2,1)S(1)} %copy-done.6, bf16[1024,1,128]{2,0,1:T(8,128)(2,1)S(1)} %bitcast.262), kind=kOutput, calls=%fused_computation.14 | convolution fusion | flops 1120990208 | bytes 19001344 | tf_op jit(solution)/shard_map/mkgd,nkd->kgmn/dot_general | solution.py:37
  227.5 9.5 %fusion.14 = f32[8,384]{1,0:T(8,128)S(1)} fusion(f32[1408,384,8]{1,0,2:T(8,128)} %get-tuple-element.40, f32[8,384]{1,0:T(8,128)S(1)} %get-tuple-element.39, pred[384,1408]{0,1:T(8,128)(4,1)S(1)} %pad_add_fusion.1), kind=kLoop, calls=%fused_computation.24 | loop fusion | flops 17298432 | bytes 17866752 | tf_op jit(solution)/shard_map/reduce_sum | solution.py:42
  237.0 9.7 %fusion.38 = bf16[384,1,8,128]{0,3,2,1:T(8,128)(2,1)S(1)} fusion(f32[1408,384,8]{1,0,2:T(8,128)} %get-tuple-element.40, f32[8,384]{1,0:T(8,128)S(1)} %get-tuple-element.39, pred[384,1408]{0,1:T(8,128)(4,1)S(1)} %pad_add_fusion.1, f32[384,8]{0,1:T(8,128)S(1)} %bitcast.276, bf16[384,1,128]{0,2,1:T(8,128)(2,1)S(1)} %copy-done.8, bf16[1024,1,128]{0,2,1:T(8,128)(2,1)} %copy.123), kind=kOutput, calls=%fused_computation.53 | convolution fusion | flops 1126105088 | bytes 19013632 | tf_op jit(solution)/shard_map/kgmn,nkd->mkgd/dot_general | solution.py:44
  248.1 7.9 %fusion.9 = (f32[8,384]{1,0:T(8,128)S(1)}, f32[1408,384,8]{1,0,2:T(8,128)}) fusion(pred[384,1408]{0,1:T(8,128)(4,1)S(1)} %pad_add_fusion, bf16[384,8,128]{0,2,1:T(8,128)(2,1)S(1)} %bitcast.257, bf16[384,1,128]{2,0,1:T(8,128)(2,1)S(1)} %copy-done.5, bf16[1024,1,128]{2,0,1:T(8,128)(2,1)S(1)} %bitcast.261), kind=kOutput, calls=%fused_computation.19 | convolution fusion | flops 1120990208 | bytes 19001344 | tf_op jit(solution)/shard_map/mkgd,nkd->kgmn/dot_general | solution.py:37
  256.0 9.4 %fusion.12 = f32[8,384]{1,0:T(8,128)S(1)} fusion(f32[1408,384,8]{1,0,2:T(8,128)} %get-tuple-element.38, f32[8,384]{1,0:T(8,128)S(1)} %get-tuple-element.37, pred[384,1408]{0,1:T(8,128)(4,1)S(1)} %pad_add_fusion), kind=kLoop, calls=%fused_computation.22 | loop fusion | flops 17298432 | bytes 17866752 | tf_op jit(solution)/shard_map/reduce_sum | solution.py:42
  265.5 9.7 %fusion.39 = bf16[384,1,8,128]{0,3,2,1:T(8,128)(2,1)S(1)} fusion(f32[1408,384,8]{1,0,2:T(8,128)} %get-tuple-element.38, f32[8,384]{1,0:T(8,128)S(1)} %get-tuple-element.37, pred[384,1408]{0,1:T(8,128)(4,1)S(1)} %pad_add_fusion, f32[384,8]{0,1:T(8,128)S(1)} %bitcast.277, bf16[384,1,128]{0,2,1:T(8,128)(2,1)S(1)} %copy-done.7, bf16[1024,1,128]{0,2,1:T(8,128)(2,1)S(1)} %copy.122), kind=kOutput, calls=%fused_computation.55 | convolution fusion | flops 1126105088 | bytes 19013632 | tf_op jit(solution)/shard_map/kgmn,nkd->mkgd/dot_general | solution.py:44
  276.7 5.6 %dynamic_update_slice.12 = bf16[1024,1024]{1,0:T(8,128)(2,1)S(1)} dynamic-update-slice(bf16[1024,1024]{1,0:T(8,128)(2,1)S(1)} %broadcast_in_dim.152, bf16[384,1024]{1,0:T(8,128)(2,1)} %broadcast_select_fusion.2, s32[]{:T(128)S(6)} %select_n.157, s32[]{:T(128)} %constant.116.clone.1) | dynamic-update-slice | bytes 1572868 | tf_op jit(solution)/shard_map/dynamic_update_slice | solution.py:105
  282.3 2.3 dynamic-slice_select_fusion.2
  284.7 5.5 %dynamic_update_slice.13 = bf16[1024,1024]{1,0:T(8,128)(2,1)S(1)} dynamic-update-slice(bf16[1024,1024]{1,0:T(8,128)(2,1)S(1)} %dynamic_update_slice.12, bf16[384,1024]{1,0:T(8,128)(2,1)} %dynamic-slice_select_fusion.2, s32[]{:T(128)S(6)} %select_n.164, s32[]{:T(128)} %constant.116.clone.1) | dynamic-update-slice | bytes 1572868 | tf_op jit(solution)/shard_map/dynamic_update_slice | solution.py:105
  290.2 2.3 dynamic-slice_select_fusion.1
  292.6 5.5 %dynamic_update_slice.14 = bf16[1024,1024]{1,0:T(8,128)(2,1)S(1)} dynamic-update-slice(bf16[1024,1024]{1,0:T(8,128)(2,1)S(1)} %dynamic_update_slice.13, bf16[384,1024]{1,0:T(8,128)(2,1)} %dynamic-slice_select_fusion.1, s32[]{:T(128)S(6)} %select_n.169, s32[]{:T(128)} %constant.116.clone.1) | dynamic-update-slice | bytes 1572868 | tf_op jit(solution)/shard_map/dynamic_update_slice | solution.py:105
  299.7 4.7 %dynamic_update_slice.15 = bf16[1024,1024]{1,0:T(8,128)(2,1)} dynamic-update-slice(bf16[1024,1024]{1,0:T(8,128)(2,1)} %copy-done, bf16[384,1024]{1,0:T(8,128)(2,1)} %dynamic-slice_select_fusion, s32[]{:T(128)S(6)} %select_n.174, s32[]{:T(128)} %constant.116.clone.1) | dynamic-update-slice | bytes 1572868 | tf_op jit(solution)/shard_map/dynamic_update_slice | solution.py:105
  (96 shorter events, 29.1 us)
Async XLA Ops:
  6.5 47.7 %copy-start.10 = (s32[4,8]{1,0:T(4,128)S(1)}, s32[4,8]{1,0:T(4,128)}, u32[]{:S(2)}) copy-start(s32[4,8]{1,0:T(4,128)} %param.10) | copy-start | bytes 388
  6.5 39.8 %copy-start.11 = (s32[1,4]{1,0:T(1,128)S(1)}, s32[1,4]{1,0:T(1,128)}, u32[]{:S(2)}) copy-start(s32[1,4]{1,0:T(1,128)} %param.13) | copy-start | bytes 52
  6.5 43.3 %copy-start.1 = (bf16[1024,1024]{1,0:T(8,128)(2,1)S(1)}, bf16[1024,1024]{1,0:T(8,128)(2,1)}, u32[]{:S(2)}) copy-start(bf16[1024,1024]{1,0:T(8,128)(2,1)} %param.7) | copy-start | bytes 6291460
  30.9 28.9 %copy-start.12 = (s32[4]{0:T(128)S(1)}, s32[4]{0:T(128)}, u32[]{:S(2)}) copy-start(s32[4]{0:T(128)} %param.12) | copy-start | bytes 52
  40.7 100.9 %all-to-all-start.1 = ((bf16[32,2,2,128,128]{4,3,2,1,0:T(8,128)(2,1)}), bf16[32,2,2,128,128]{4,3,2,1,0:T(8,128)(2,1)}, u32[]{:S(2)}, u32[]{:S(2)}) async-start(bf16[32,2,2,128,128]{4,3,2,1,0:T(8,128)(2,1)} %broadcast_select_fusion), calls=%async_computation.1 | async-start | bytes 8388608 | tf_op jit(solution)/shard_map/all_to_all | solution.py:60
  45.6 37.5 %all-gather.2.cloned.1.call-start = ((), (), s32[]{:S(2)}) async-start(), calls=%async_computation.2 | async-start | bytes 4718592 | tf_op jit(solution)/shard_map/all_gather | solution.py:57
  185.2 19.4 %copy-start.9 = (bf16[384,1,128]{0,2,1:T(8,128)(2,1)S(1)}, bf16[384,1,128]{0,2,1:T(8,128)(2,1)}, u32[]{:S(2)}) copy-start(bf16[384,1,128]{0,2,1:T(8,128)(2,1)} %copy.103) | copy-start | bytes 294916
  204.6 13.2 %copy-start.4 = (bf16[1,8,1,128,128]{4,3,2,1,0:T(8,128)(2,1)S(1)}, bf16[1,8,1,128,128]{4,3,2,1,0:T(8,128)(2,1)}, u32[]{:S(2)}) copy-start(bf16[1,8,1,128,128]{4,3,2,1,0:T(8,128)(2,1)} %get-tuple-element.18) | copy-start | bytes 786436
  204.6 14.0 %copy-start.6 = (bf16[384,1,128]{2,0,1:T(8,128)(2,1)S(1)}, bf16[384,1,128]{2,0,1:T(8,128)(2,1)}, u32[]{:S(2)}) copy-start(bf16[384,1,128]{2,0,1:T(8,128)(2,1)} %get-tuple-element.11) | copy-start | bytes 294916
  227.5 9.5 %copy-start.8 = (bf16[384,1,128]{0,2,1:T(8,128)(2,1)S(1)}, bf16[384,1,128]{0,2,1:T(8,128)(2,1)}, u32[]{:S(2)}) copy-start(bf16[384,1,128]{0,2,1:T(8,128)(2,1)} %copy.97) | copy-start | bytes 294916
  237.0 11.0 %copy-start.3 = (bf16[1,8,1,128,128]{4,3,2,1,0:T(8,128)(2,1)S(1)}, bf16[1,8,1,128,128]{4,3,2,1,0:T(8,128)(2,1)}, u32[]{:S(2)}) copy-start(bf16[1,8,1,128,128]{4,3,2,1,0:T(8,128)(2,1)} %get-tuple-element.20) | copy-start | bytes 786436
  237.0 11.1 %copy-start.5 = (bf16[384,1,128]{2,0,1:T(8,128)(2,1)S(1)}, bf16[384,1,128]{2,0,1:T(8,128)(2,1)}, u32[]{:S(2)}) copy-start(bf16[384,1,128]{2,0,1:T(8,128)(2,1)} %get-tuple-element.12) | copy-start | bytes 294916
  248.1 17.4 %copy-start.7 = (bf16[384,1,128]{0,2,1:T(8,128)(2,1)S(1)}, bf16[384,1,128]{0,2,1:T(8,128)(2,1)}, u32[]{:S(2)}) copy-start(bf16[384,1,128]{0,2,1:T(8,128)(2,1)} %copy.91) | copy-start | bytes 294916
  265.5 32.7 %copy-start.2 = (bf16[384,1024]{1,0:T(8,128)(2,1)S(1)}, bf16[384,1024]{1,0:T(8,128)(2,1)}, u32[]{:S(2)}) copy-start(bf16[384,1024]{1,0:T(8,128)(2,1)} %copy.113) | copy-start | bytes 2359300
  298.1 1.6 copy-start
Sparse Core Ops, SparseCore 0:
  48.3 34.8 all-gather.1
where the time goes:
time: 315 us; the launch traced here: 311 us
  matrix products  77.5 us (25%)
  waiting for transfers between devices  63.6 us (20%)
  local copies, waits for them, and re-layouts  62.7 us (20%)
  other arithmetic  60 us (19%)
  between operations  21.5 us (7%)
  blocking collectives  21.1 us (7%)
  starting transfers between devices  5.07 us (2%)
    all_to_all x1, waiting for transfers between devices, local(): lax.all_to_all(jnp.take(page_pool, lax.all_to_all(buffer, 'store', split_...  52.7 us
    dot_general x4, matrix products, attend(): jnp.einsum('kgmn,nkd->mkgd', rounded, value_rows, preferred_element_type=...  40.9 us
    reduce_sum x4, other arithmetic, attend(): row_total = jnp.sum(weights, axis=-1)  38.1 us
    dot_general x4, matrix products, attend(): jnp.einsum('mkgd,nkd->kgmn', q_rows, key_rows, preferred_element_type=jnp...  36.7 us
    dynamic_update_slice x4, local copies, waits for them, and re-layouts, local(): lax.dynamic_update_slice_in_dim(output, jnp.where(row_ok[:, None], mixed_...  21.4 us
    all_to_all x1, blocking collectives, local(): lax.all_to_all(buffer, 'store', split_axis=0, concat_axis=0, tiled=True)  21.1 us
    all_gather x1, waiting for transfers between devices, local(): gathered = lax.all_gather(fresh_kv, 'tp', axis=1, tiled=True)  10.4 us
    unnamed x30, local copies, waits for them, and re-layouts  7.46 us
  transfers between devices with their start and end apart: 2, of which 2 were waited for; matrix products, arithmetic and copies ran while one was open for 8% of the time, Pallas kernels for 0%

commit v1 on v0

--- a/solution.py
+++ b/solution.py
@@ -9,6 +9,23 @@
 PAGE = 128
 PAGES_MAX = 8
 MOST_NEW = 384
+
+
+def pass_gates(mine_x, shard_axis="tp"):
+    total_devices = lax.axis_size(shard_axis)
+    q_next = sorted(((t, (t + 1) % total_devices) for t in range(total_devices)))
+    out_arr = mine_x
+    column = [out_arr]
+    j0 = 1
+    while j0 < total_devices:
+        out_arr = lax.ppermute(out_arr, perm=q_next, axis_name=shard_axis)
+        column.insert(0, out_arr)
+        j0 += 1
+    return jnp.roll(
+        jnp.concatenate(column, axis=1),
+        shift=(lax.axis_index(shard_axis) + 1) * mine_x.shape[1],
+        axis=1,
+    )
 
 
 def plan_requests(owners, slot_ids, prefix, stores, capacity):
@@ -54,7 +71,7 @@
     kv_local = head_width // HD
     group_size = queries.shape[1] // head_width
     capacity = max(2, (REQ_HOST * PAGES_MAX + stores - 1) // stores)
-    gathered = lax.all_gather(fresh_kv, "tp", axis=1, tiled=True)
+    gathered = pass_gates(fresh_kv)
     new_kv = lax.dynamic_slice_in_dim(gathered, lax.axis_index("tp") * head_width, head_width, 2)
     buffer, position = plan_requests(page_host, page_slot, prefix_len, stores, capacity)
     arrived = lax.all_to_all(

time: 315 us -> 305 us (0.968)
  waiting for transfers between devices: 63.6 us -> 45.8 us
  between operations: 21.5 us -> 8.24 us
  local copies, waits for them, and re-layouts: 62.7 us -> 75.1 us
  other arithmetic: 60 us -> 63.2 us
  starting transfers between devices: 5.07 us -> 8.26 us
    all_to_all x1, waiting for transfers between devices: 52.7 us -> 12.6 us  [local(): lax.all_to_all(jnp.take(page_pool, lax.all_to_all(buffer, 'store', split_...]
    ppermute x0 -> x7, waiting for transfers between devices: none -> 33.2 us  [pass_gates(): out_arr = lax.ppermute(out_arr, perm=q_next, axis_name=shard_axis)]
    unnamed x30 -> x55, local copies, waits for them, and re-layouts: 7.46 us -> 20.1 us
    all_gather x1 -> x0, waiting for transfers between devices: 10.4 us -> none  [local(): gathered = lax.all_gather(fresh_kv, 'tp', axis=1, tiled=True)]
    ppermute x0 -> x7, starting transfers between devices: none -> 3.23 us  [pass_gates(): out_arr = lax.ppermute(out_arr, perm=q_next, axis_name=shard_axis)]
  transfers between devices with their start and end apart: 2 -> 8, of which waited for: 2 -> 6; matrix products, arithmetic and copies ran while one was open for 8% -> 13% of each run, Pallas kernels for 0% -> 0%
where the time goes in v1:
time: 305 us; the launch traced here: 300 us
  matrix products  78.4 us (26%)
  local copies, waits for them, and re-layouts  75.1 us (25%)
  other arithmetic  63.2 us (21%)
  waiting for transfers between devices  45.8 us (15%)
  blocking collectives  21.1 us (7%)
  starting transfers between devices  8.26 us (3%)
  between operations  8.24 us (3%)
    dot_general x4, matrix products, attend(): jnp.einsum('kgmn,nkd->mkgd', rounded, value_rows, preferred_element_type=...  41.7 us
    reduce_sum x4, other arithmetic, attend(): row_total = jnp.sum(weights, axis=-1)  38.2 us
    dot_general x4, matrix products, attend(): jnp.einsum('mkgd,nkd->kgmn', q_rows, key_rows, preferred_element_type=jnp...  36.7 us
    ppermute x7, waiting for transfers between devices, pass_gates(): out_arr = lax.ppermute(out_arr, perm=q_next, axis_name=shard_axis)  33.2 us
    dynamic_update_slice x4, local copies, waits for them, and re-layouts, local(): lax.dynamic_update_slice_in_dim(output, jnp.where(row_ok[:, None], mixed_...  21.4 us
    all_to_all x1, blocking collectives, local(): lax.all_to_all(buffer, 'store', split_axis=0, concat_axis=0, tiled=True)  21.1 us
    unnamed x55, local copies, waits for them, and re-layouts  20.1 us
    all_to_all x1, waiting for transfers between devices, local(): lax.all_to_all(jnp.take(page_pool, lax.all_to_all(buffer, 'store', split_...  12.6 us
  transfers between devices with their start and end apart: 8, of which 6 were waited for; matrix products, arithmetic and copies ran while one was open for 13% of the time, Pallas kernels for 0%

profile of v1, /device:TPU:2, one launch (start us, length us, event | category | flops | bytes accessed | tf_op | source)
XLA Modules:
  0.0 300.1 jit_solution(17667374048298610260)
XLA Ops:
  2.8 21.1 %all_to_all.20 = s32[32,1,2]{2,1,0:T(1,128)S(1)} all-to-all(s32[32,1,2]{2,1,0:T(1,128)S(1)} %bitcast.273), channel_id=1, replica_groups=mesh['store'=32,'tp'=8] {'store'}, dimensions={0} | all-to-all | bytes 512 | tf_op jit(solution)/shard_map/all_to_all | solution.py:80
  24.2 5.3 %gather_fusion = bf16[64,2,128,128]{3,2,1,0:T(8,128)(2,1)} fusion(bf16[64,2,128,128]{3,2,1,0:T(8,128)(2,1)} %param.9, s32[1024]{0:T(1024)S(1)} %pad_clamp_fusion.1), kind=kCustom, calls=%fused_computation | custom fusion | bytes 8388864 | tf_op jit(solution)/shard_map/jit(_take)/gather | solution.py:78
  29.5 4.7 %broadcast_select_fusion = bf16[32,2,2,128,128]{4,3,2,1,0:T(8,128)(2,1)} fusion(bf16[32,2,2,128,128]{4,3,2,1,0:T(8,128)(2,1)} %bitcast.255, pred[32,2]{1,0:T(8,128)(4,1)S(1)} %copy.87), kind=kLoop, calls=%fused_computation.42 | loop fusion | flops 2097152 | bytes 8388672 | tf_op jit(solution)/shard_map/jit(_take)/select_n | solution.py:78
  34.2 5.0 %all-to-all-start.1 = ((bf16[32,2,2,128,128]{4,3,2,1,0:T(8,128)(2,1)}), bf16[32,2,2,128,128]{4,3,2,1,0:T(8,128)(2,1)}, u32[]{:S(2)}, u32[]{:S(2)}) async-start(bf16[32,2,2,128,128]{4,3,2,1,0:T(8,128)(2,1)} %broadcast_select_fusion), calls=%async_computation.1 | async-start | bytes 8388608 | tf_op jit(solution)/shard_map/all_to_all | solution.py:77
  55.7 6.3 %collective-permute-done.1 = bf16[2,128,1024]{2,1,0:T(8,128)(2,1)S(1)} collective-permute-done((bf16[2,128,1024]{2,1,0:T(8,128)(2,1)}, bf16[2,128,1024]{2,1,0:T(8,128)(2,1)S(1)}, u32[]{:S(2)}, u32[]{:S(2)}) %collective-permute-start.1) | collective-permute-done | bytes 524320 | tf_op jit(solution)/shard_map/ppermute | solution.py:21
  64.4 6.2 %collective-permute-done.2 = bf16[2,128,1024]{2,1,0:T(8,128)(2,1)S(1)} collective-permute-done((bf16[2,128,1024]{2,1,0:T(8,128)(2,1)S(1)}, bf16[2,128,1024]{2,1,0:T(8,128)(2,1)S(1)}, u32[]{:S(2)}, u32[]{:S(2)}) %collective-permute-start.2) | collective-permute-done | bytes 524320 | tf_op jit(solution)/shard_map/ppermute | solution.py:21
  71.6 7.7 %collective-permute-done.3 = bf16[2,128,1024]{2,1,0:T(8,128)(2,1)S(1)} collective-permute-done((bf16[2,128,1024]{2,1,0:T(8,128)(2,1)S(1)}, bf16[2,128,1024]{2,1,0:T(8,128)(2,1)S(1)}, u32[]{:S(2)}, u32[]{:S(2)}) %collective-permute-start.3) | collective-permute-done | bytes 524320 | tf_op jit(solution)/shard_map/ppermute | solution.py:21
  80.9 7.1 %collective-permute-done.4 = bf16[2,128,1024]{2,1,0:T(8,128)(2,1)} collective-permute-done((bf16[2,128,1024]{2,1,0:T(8,128)(2,1)S(1)}, bf16[2,128,1024]{2,1,0:T(8,128)(2,1)}, u32[]{:S(2)}, u32[]{:S(2)}) %collective-permute-start.4) | collective-permute-done | bytes 524320 | tf_op jit(solution)/shard_map/ppermute | solution.py:21
  88.6 2.3 copy.129
  90.9 2.3 copy.128
  99.9 5.9 %collective-permute-done.6 = bf16[2,128,1024]{2,1,0:T(8,128)(2,1)S(1)} collective-permute-done((bf16[2,128,1024]{2,1,0:T(8,128)(2,1)}, bf16[2,128,1024]{2,1,0:T(8,128)(2,1)S(1)}, u32[]{:S(2)}, u32[]{:S(2)}) %collective-permute-start.6) | collective-permute-done | bytes 524320 | tf_op jit(solution)/shard_map/ppermute | solution.py:21
  122.5 12.6 %all-to-all-done.1 = bf16[32,2,2,128,128]{4,3,2,1,0:T(8,128)(2,1)} async-done(((bf16[32,2,2,128,128]{4,3,2,1,0:T(8,128)(2,1)}), bf16[32,2,2,128,128]{4,3,2,1,0:T(8,128)(2,1)}, u32[]{:S(2)}, u32[]{:S(2)}) %all-to-all-start.1) | async-done | bytes 4194336 | tf_op jit(solution)/shard_map/all_to_all | solution.py:77
  135.1 4.3 %gather_fusion.1 = bf16[32,2,128,128]{3,2,1,0:T(8,128)(2,1)} fusion(bf16[64,2,128,128]{3,2,1,0:T(8,128)(2,1)} %bitcast.9, s32[1024]{0:T(1024)S(1)} %pad_clamp_fusion), kind=kCustom, calls=%fused_computation.1 | custom fusion | bytes 4194432 | tf_op jit(solution)/shard_map/jit(_take)/gather | solution.py:89
  144.2 9.9 %fusion = (f32[8,384]{1,0:T(8,128)S(1)}, f32[1408,384,8]{1,0,2:T(8,128)}) fusion(pred[384,1408]{0,1:T(8,128)(4,1)S(1)} %pad_add_fusion.3, bf16[384,8,128]{0,2,1:T(8,128)(2,1)} %bitcast.260, bf16[384,1,128]{2,0,1:T(8,128)(2,1)} %get-tuple-element.9, bf16[1024,1,128]{2,0,1:T(8,128)(2,1)} %bitcast.264), kind=kOutput, calls=%fused_computation.4 | convolution fusion | flops 1120990208 | bytes 19001344 | tf_op jit(solution)/shard_map/mkgd,nkd->kgmn/dot_general | solution.py:54
  154.2 9.8 %fusion.18 = f32[8,384]{1,0:T(8,128)S(1)} fusion(f32[1408,384,8]{1,0,2:T(8,128)} %get-tuple-element.44, f32[8,384]{1,0:T(8,128)S(1)} %get-tuple-element.43, pred[384,1408]{0,1:T(8,128)(4,1)S(1)} %pad_add_fusion.3), kind=kLoop, calls=%fused_computation.28 | loop fusion | flops 17298432 | bytes 17866752 | tf_op jit(solution)/shard_map/reduce_sum | solution.py:59
  164.0 10.6 %fusion.36 = bf16[384,1,8,128]{0,3,2,1:T(8,128)(2,1)} fusion(f32[1408,384,8]{1,0,2:T(8,128)} %get-tuple-element.44, f32[8,384]{1,0:T(8,128)S(1)} %get-tuple-element.43, pred[384,1408]{0,1:T(8,128)(4,1)S(1)} %pad_add_fusion.3, f32[384,8]{0,1:T(8,128)S(1)} %bitcast.274, bf16[384,1,128]{0,2,1:T(8,128)(2,1)} %copy.109, bf16[1024,1,128]{0,2,1:T(8,128)(2,1)} %copy.125), kind=kOutput, calls=%fused_computation.49 | convolution fusion | flops 1126105088 | bytes 19013632 | tf_op jit(solution)/shard_map/kgmn,nkd->mkgd/dot_general | solution.py:61
  178.7 9.9 %fusion.3 = (f32[8,384]{1,0:T(8,128)S(1)}, f32[1408,384,8]{1,0,2:T(8,128)}) fusion(pred[384,1408]{0,1:T(8,128)(4,1)S(1)} %pad_add_fusion.2, bf16[384,8,128]{0,2,1:T(8,128)(2,1)} %bitcast.259, bf16[384,1,128]{2,0,1:T(8,128)(2,1)} %get-tuple-element.10, bf16[1024,1,128]{2,0,1:T(8,128)(2,1)} %bitcast.263), kind=kOutput, calls=%fused_computation.9 | convolution fusion | flops 1120990208 | bytes 19001344 | tf_op jit(solution)/shard_map/mkgd,nkd->kgmn/dot_general | solution.py:54
  188.7 9.5 %fusion.16 = f32[8,384]{1,0:T(8,128)S(1)} fusion(f32[1408,384,8]{1,0,2:T(8,128)} %get-tuple-element.42, f32[8,384]{1,0:T(8,128)S(1)} %get-tuple-element.41, pred[384,1408]{0,1:T(8,128)(4,1)S(1)} %pad_add_fusion.2), kind=kLoop, calls=%fused_computation.26 | loop fusion | flops 17298432 | bytes 17866752 | tf_op jit(solution)/shard_map/reduce_sum | solution.py:59
  198.1 10.8 %fusion.37 = bf16[384,1,8,128]{0,3,2,1:T(8,128)(2,1)} fusion(f32[1408,384,8]{1,0,2:T(8,128)} %get-tuple-element.42, f32[8,384]{1,0:T(8,128)S(1)} %get-tuple-element.41, pred[384,1408]{0,1:T(8,128)(4,1)S(1)} %pad_add_fusion.2, f32[384,8]{0,1:T(8,128)S(1)} %bitcast.275, bf16[384,1,128]{0,2,1:T(8,128)(2,1)S(1)} %copy-done.14, bf16[1024,1,128]{0,2,1:T(8,128)(2,1)} %copy.124), kind=kOutput, calls=%fused_computation.51 | convolution fusion | flops 1126105088 | bytes 19013632 | tf_op jit(solution)/shard_map/kgmn,nkd->mkgd/dot_general | solution.py:61
  208.9 2.3 copy.107
  212.1 8.9 %fusion.6 = (f32[8,384]{1,0:T(8,128)S(1)}, f32[1408,384,8]{1,0,2:T(8,128)}) fusion(pred[384,1408]{0,1:T(8,128)(4,1)S(1)} %pad_add_fusion.1, bf16[384,8,128]{0,2,1:T(8,128)(2,1)} %bitcast.258, bf16[384,1,128]{2,0,1:T(8,128)(2,1)S(1)} %copy-done.11, bf16[1024,1,128]{2,0,1:T(8,128)(2,1)S(1)} %bitcast.262), kind=kOutput, calls=%fused_computation.14 | convolution fusion | flops 1120990208 | bytes 19001344 | tf_op jit(solution)/shard_map/mkgd,nkd->kgmn/dot_general | solution.py:54
  221.0 9.5 %fusion.14 = f32[8,384]{1,0:T(8,128)S(1)} fusion(f32[1408,384,8]{1,0,2:T(8,128)} %get-tuple-element.40, f32[8,384]{1,0:T(8,128)S(1)} %get-tuple-element.39, pred[384,1408]{0,1:T(8,128)(4,1)S(1)} %pad_add_fusion.1), kind=kLoop, calls=%fused_computation.24 | loop fusion | flops 17298432 | bytes 17866752 | tf_op jit(solution)/shard_map/reduce_sum | solution.py:59
  230.5 9.7 %fusion.38 = bf16[384,1,8,128]{0,3,2,1:T(8,128)(2,1)S(1)} fusion(f32[1408,384,8]{1,0,2:T(8,128)} %get-tuple-element.40, f32[8,384]{1,0:T(8,128)S(1)} %get-tuple-element.39, pred[384,1408]{0,1:T(8,128)(4,1)S(1)} %pad_add_fusion.1, f32[384,8]{0,1:T(8,128)S(1)} %bitcast.276, bf16[384,1,128]{0,2,1:T(8,128)(2,1)S(1)} %copy-done.13, bf16[1024,1,128]{0,2,1:T(8,128)(2,1)} %copy.123), kind=kOutput, calls=%fused_computation.53 | convolution fusion | flops 1126105088 | bytes 19013632 | tf_op jit(solution)/shard_map/kgmn,nkd->mkgd/dot_general | solution.py:61
  241.6 7.9 %fusion.9 = (f32[8,384]{1,0:T(8,128)S(1)}, f32[1408,384,8]{1,0,2:T(8,128)}) fusion(pred[384,1408]{0,1:T(8,128)(4,1)S(1)} %pad_add_fusion, bf16[384,8,128]{0,2,1:T(8,128)(2,1)S(1)} %bitcast.257, bf16[384,1,128]{2,0,1:T(8,128)(2,1)S(1)} %copy-done.10, bf16[1024,1,128]{2,0,1:T(8,128)(2,1)S(1)} %bitcast.261), kind=kOutput, calls=%fused_computation.19 | convolution fusion | flops 1120990208 | bytes 19001344 | tf_op jit(solution)/shard_map/mkgd,nkd->kgmn/dot_general | solution.py:54
  249.5 9.5 %fusion.12 = f32[8,384]{1,0:T(8,128)S(1)} fusion(f32[1408,384,8]{1,0,2:T(8,128)} %get-tuple-element.38, f32[8,384]{1,0:T(8,128)S(1)} %get-tuple-element.37, pred[384,1408]{0,1:T(8,128)(4,1)S(1)} %pad_add_fusion), kind=kLoop, calls=%fused_computation.22 | loop fusion | flops 17298432 | bytes 17866752 | tf_op jit(solution)/shard_map/reduce_sum | solution.py:59
  259.0 10.5 %fusion.39 = bf16[384,1,8,128]{0,3,2,1:T(8,128)(2,1)} fusion(f32[1408,384,8]{1,0,2:T(8,128)} %get-tuple-element.38, f32[8,384]{1,0:T(8,128)S(1)} %get-tuple-element.37, pred[384,1408]{0,1:T(8,128)(4,1)S(1)} %pad_add_fusion, f32[384,8]{0,1:T(8,128)S(1)} %bitcast.277, bf16[384,1,128]{0,2,1:T(8,128)(2,1)S(1)} %copy-done.12, bf16[1024,1,128]{0,2,1:T(8,128)(2,1)S(1)} %copy.122), kind=kOutput, calls=%fused_computation.55 | convolution fusion | flops 1126105088 | bytes 19013632 | tf_op jit(solution)/shard_map/kgmn,nkd->mkgd/dot_general | solution.py:61
  272.2 5.6 %dynamic_update_slice.12 = bf16[1024,1024]{1,0:T(8,128)(2,1)S(1)} dynamic-update-slice(bf16[1024,1024]{1,0:T(8,128)(2,1)S(1)} %broadcast_in_dim.152, bf16[384,1024]{1,0:T(8,128)(2,1)} %broadcast_select_fusion.2, s32[]{:T(128)S(6)} %select_n.172, s32[]{:T(128)} %constant.145.clone.1) | dynamic-update-slice | bytes 1572868 | tf_op jit(solution)/shard_map/dynamic_update_slice | solution.py:122
  277.8 2.3 dynamic-slice_select_fusion.2
  280.2 5.5 %dynamic_update_slice.13 = bf16[1024,1024]{1,0:T(8,128)(2,1)S(1)} dynamic-update-slice(bf16[1024,1024]{1,0:T(8,128)(2,1)S(1)} %dynamic_update_slice.12, bf16[384,1024]{1,0:T(8,128)(2,1)} %dynamic-slice_select_fusion.2, s32[]{:T(128)S(6)} %select_n.182, s32[]{:T(128)} %constant.145.clone.1) | dynamic-update-slice | bytes 1572868 | tf_op jit(solution)/shard_map/dynamic_update_slice | solution.py:122
  285.7 2.3 dynamic-slice_select_fusion.1
  288.1 5.5 %dynamic_update_slice.14 = bf16[1024,1024]{1,0:T(8,128)(2,1)S(1)} dynamic-update-slice(bf16[1024,1024]{1,0:T(8,128)(2,1)S(1)} %dynamic_update_slice.13, bf16[384,1024]{1,0:T(8,128)(2,1)} %dynamic-slice_select_fusion.1, s32[]{:T(128)S(6)} %select_n.187, s32[]{:T(128)} %constant.145.clone.1) | dynamic-update-slice | bytes 1572868 | tf_op jit(solution)/shard_map/dynamic_update_slice | solution.py:122
  295.2 4.7 %dynamic_update_slice.15 = bf16[1024,1024]{1,0:T(8,128)(2,1)} dynamic-update-slice(bf16[1024,1024]{1,0:T(8,128)(2,1)} %copy-done, bf16[384,1024]{1,0:T(8,128)(2,1)} %dynamic-slice_select_fusion, s32[]{:T(128)S(6)} %select_n.192, s32[]{:T(128)} %constant.145.clone.1) | dynamic-update-slice | bytes 1572868 | tf_op jit(solution)/shard_map/dynamic_update_slice | solution.py:122
  (133 shorter events, 56.1 us)
Async XLA Ops:
  29.5 9.8 %copy-start.3 = (bf16[2,128,1024]{2,1,0:T(8,128)(2,1)S(1)}, bf16[2,128,1024]{2,1,0:T(8,128)(2,1)}, u32[]{:S(2)}) copy-start(bf16[2,128,1024]{2,1,0:T(8,128)(2,1)} %param.8) | copy-start | bytes 1572868
  29.5 9.8 %copy-start.16 = (s32[1,4]{1,0:T(1,128)S(1)}, s32[1,4]{1,0:T(1,128)}, u32[]{:S(2)}) copy-start(s32[1,4]{1,0:T(1,128)} %param.13) | copy-start | bytes 52
  29.5 13.3 %copy-start.15 = (s32[4,8]{1,0:T(4,128)S(1)}, s32[4,8]{1,0:T(4,128)}, u32[]{:S(2)}) copy-start(s32[4,8]{1,0:T(4,128)} %param.10) | copy-start | bytes 388
  29.5 18.9 %copy-start.17 = (s32[4]{0:T(128)S(1)}, s32[4]{0:T(128)}, u32[]{:S(2)}) copy-start(s32[4]{0:T(128)} %param.12) | copy-start | bytes 52
  29.5 20.9 %copy-start.1 = (bf16[1024,1024]{1,0:T(8,128)(2,1)S(1)}, bf16[1024,1024]{1,0:T(8,128)(2,1)}, u32[]{:S(2)}) copy-start(bf16[1024,1024]{1,0:T(8,128)(2,1)} %param.7) | copy-start | bytes 6291460
  34.2 100.9 %all-to-all-start.1 = ((bf16[32,2,2,128,128]{4,3,2,1,0:T(8,128)(2,1)}), bf16[32,2,2,128,128]{4,3,2,1,0:T(8,128)(2,1)}, u32[]{:S(2)}, u32[]{:S(2)}) async-start(bf16[32,2,2,128,128]{4,3,2,1,0:T(8,128)(2,1)} %broadcast_select_fusion), calls=%async_computation.1 | async-start | bytes 8388608 | tf_op jit(solution)/shard_map/all_to_all | solution.py:77
  39.3 13.9 %collective-permute-start = (bf16[2,128,1024]{2,1,0:T(8,128)(2,1)S(1)}, bf16[2,128,1024]{2,1,0:T(8,128)(2,1)}, u32[]{:S(2)}, u32[]{:S(2)}) collective-permute-start(bf16[2,128,1024]{2,1,0:T(8,128)(2,1)S(1)} %copy-done.3), channel_id=1, source_target_pairs={{0,1},{1,2},{2,3},{3,4},{4,5},{5,6},{6,7},{7,0},{8,9},{9,10},{10,1... | collective-permute-start | bytes 1572872 | tf_op jit(solution)/shard_map/ppermute | solution.py:21
  53.2 8.8 %collective-permute-start.1 = (bf16[2,128,1024]{2,1,0:T(8,128)(2,1)}, bf16[2,128,1024]{2,1,0:T(8,128)(2,1)S(1)}, u32[]{:S(2)}, u32[]{:S(2)}) collective-permute-start(bf16[2,128,1024]{2,1,0:T(8,128)(2,1)} %collective-permute-done), channel_id=1, source_target_pairs={{0,1},{1,2},{2,3},{3,4},{4,5},{5,6},{6,7},{7,0},{8,9},{9,10},{10,1... | collective-permute-start | bytes 1572872 | tf_op jit(solution)/shard_map/ppermute | solution.py:21
  62.0 9.3 %copy-start.4 = (bf16[2,128,1024]{2,1,0:T(8,128)(2,1)}, bf16[2,128,1024]{2,1,0:T(8,128)(2,1)S(1)}, u32[]{:S(2)}) copy-start(bf16[2,128,1024]{2,1,0:T(8,128)(2,1)S(1)} %collective-permute-done.1) | copy-start | bytes 1572868
  62.0 8.6 %collective-permute-start.2 = (bf16[2,128,1024]{2,1,0:T(8,128)(2,1)S(1)}, bf16[2,128,1024]{2,1,0:T(8,128)(2,1)S(1)}, u32[]{:S(2)}, u32[]{:S(2)}) collective-permute-start(bf16[2,128,1024]{2,1,0:T(8,128)(2,1)S(1)} %collective-permute-done.1), channel_id=1, source_target_pairs={{0,1},{1,2},{2,3},{3,4},{4,5},{5,6},{6,7},{7,0},{8,9},{9,10},{10,1... | collective-permute-start | bytes 1572872 | tf_op jit(solution)/shard_map/ppermute | solution.py:21
  70.6 28.0 %copy-start.5 = (bf16[2,128,1024]{2,1,0:T(8,128)(2,1)}, bf16[2,128,1024]{2,1,0:T(8,128)(2,1)S(1)}, u32[]{:S(2)}) copy-start(bf16[2,128,1024]{2,1,0:T(8,128)(2,1)S(1)} %collective-permute-done.2) | copy-start | bytes 1572868
  70.6 8.6 %collective-permute-start.3 = (bf16[2,128,1024]{2,1,0:T(8,128)(2,1)S(1)}, bf16[2,128,1024]{2,1,0:T(8,128)(2,1)S(1)}, u32[]{:S(2)}, u32[]{:S(2)}) collective-permute-start(bf16[2,128,1024]{2,1,0:T(8,128)(2,1)S(1)} %collective-permute-done.2), channel_id=1, source_target_pairs={{0,1},{1,2},{2,3},{3,4},{4,5},{5,6},{6,7},{7,0},{8,9},{9,10},{10,1... | collective-permute-start | bytes 1572872 | tf_op jit(solution)/shard_map/ppermute | solution.py:21
  79.3 0.8 copy-start.7
  79.3 8.7 %collective-permute-start.4 = (bf16[2,128,1024]{2,1,0:T(8,128)(2,1)S(1)}, bf16[2,128,1024]{2,1,0:T(8,128)(2,1)}, u32[]{:S(2)}, u32[]{:S(2)}) collective-permute-start(bf16[2,128,1024]{2,1,0:T(8,128)(2,1)S(1)} %collective-permute-done.3), channel_id=1, source_target_pairs={{0,1},{1,2},{2,3},{3,4},{4,5},{5,6},{6,7},{7,0},{8,9},{9,10},{10,1... | collective-permute-start | bytes 1572872 | tf_op jit(solution)/shard_map/ppermute | solution.py:21
  88.0 9.1 %collective-permute-start.5 = (bf16[2,128,1024]{2,1,0:T(8,128)(2,1)}, bf16[2,128,1024]{2,1,0:T(8,128)(2,1)}, u32[]{:S(2)}, u32[]{:S(2)}) collective-permute-start(bf16[2,128,1024]{2,1,0:T(8,128)(2,1)} %collective-permute-done.4), channel_id=1, source_target_pairs={{0,1},{1,2},{2,3},{3,4},{4,5},{5,6},{6,7},{7,0},{8,9},{9,10},{10,1... | collective-permute-start | bytes 1572872 | tf_op jit(solution)/shard_map/ppermute | solution.py:21
  97.1 8.8 %collective-permute-start.6 = (bf16[2,128,1024]{2,1,0:T(8,128)(2,1)}, bf16[2,128,1024]{2,1,0:T(8,128)(2,1)S(1)}, u32[]{:S(2)}, u32[]{:S(2)}) collective-permute-start(bf16[2,128,1024]{2,1,0:T(8,128)(2,1)} %collective-permute-done.5), channel_id=1, source_target_pairs={{0,1},{1,2},{2,3},{3,4},{4,5},{5,6},{6,7},{7,0},{8,9},{9,10},{10,1... | collective-permute-start | bytes 1572872 | tf_op jit(solution)/shard_map/ppermute | solution.py:21
  98.7 17.1 %copy-start.6 = (bf16[2,128,1024]{2,1,0:T(8,128)(2,1)S(1)}, bf16[2,128,1024]{2,1,0:T(8,128)(2,1)}, u32[]{:S(2)}) copy-start(bf16[2,128,1024]{2,1,0:T(8,128)(2,1)} %copy-done.5) | copy-start | bytes 1572868
  188.7 9.5 %copy-start.14 = (bf16[384,1,128]{0,2,1:T(8,128)(2,1)S(1)}, bf16[384,1,128]{0,2,1:T(8,128)(2,1)}, u32[]{:S(2)}) copy-start(bf16[384,1,128]{0,2,1:T(8,128)(2,1)} %copy.103) | copy-start | bytes 294916
  198.1 13.1 %copy-start.9 = (bf16[1,8,1,128,128]{4,3,2,1,0:T(8,128)(2,1)S(1)}, bf16[1,8,1,128,128]{4,3,2,1,0:T(8,128)(2,1)}, u32[]{:S(2)}) copy-start(bf16[1,8,1,128,128]{4,3,2,1,0:T(8,128)(2,1)} %get-tuple-element.18) | copy-start | bytes 786436
  198.1 14.0 %copy-start.11 = (bf16[384,1,128]{2,0,1:T(8,128)(2,1)S(1)}, bf16[384,1,128]{2,0,1:T(8,128)(2,1)}, u32[]{:S(2)}) copy-start(bf16[384,1,128]{2,0,1:T(8,128)(2,1)} %get-tuple-element.11) | copy-start | bytes 294916
  221.0 9.5 %copy-start.13 = (bf16[384,1,128]{0,2,1:T(8,128)(2,1)S(1)}, bf16[384,1,128]{0,2,1:T(8,128)(2,1)}, u32[]{:S(2)}) copy-start(bf16[384,1,128]{0,2,1:T(8,128)(2,1)} %copy.97) | copy-start | bytes 294916
  230.5 11.0 %copy-start.8 = (bf16[1,8,1,128,128]{4,3,2,1,0:T(8,128)(2,1)S(1)}, bf16[1,8,1,128,128]{4,3,2,1,0:T(8,128)(2,1)}, u32[]{:S(2)}) copy-start(bf16[1,8,1,128,128]{4,3,2,1,0:T(8,128)(2,1)} %get-tuple-element.20) | copy-start | bytes 786436
  230.5 11.1 %copy-start.10 = (bf16[384,1,128]{2,0,1:T(8,128)(2,1)S(1)}, bf16[384,1,128]{2,0,1:T(8,128)(2,1)}, u32[]{:S(2)}) copy-start(bf16[384,1,128]{2,0,1:T(8,128)(2,1)} %get-tuple-element.12) | copy-start | bytes 294916
  249.5 9.5 %copy-start.12 = (bf16[384,1,128]{0,2,1:T(8,128)(2,1)S(1)}, bf16[384,1,128]{0,2,1:T(8,128)(2,1)}, u32[]{:S(2)}) copy-start(bf16[384,1,128]{0,2,1:T(8,128)(2,1)} %copy.91) | copy-start | bytes 294916
  269.5 24.2 %copy-start.2 = (bf16[384,1024]{1,0:T(8,128)(2,1)S(1)}, bf16[384,1024]{1,0:T(8,128)(2,1)}, u32[]{:S(2)}) copy-start(bf16[384,1024]{1,0:T(8,128)(2,1)} %copy.113) | copy-start | bytes 2359300
  293.6 1.6 copy-start
